TPU v7x, 32 devices: a whole 2x2x4 slice. The times are simulated.
32 devices in a mesh: section: 2 (over core), dp: 16 (over z, y, x).
Axes of the slice: x: 2, y: 2, z: 4, core: 2. Of those that a mesh axis runs over, the one named last changes fastest.
Arguments:
- inputs: bfloat16 [2, 16, 256, 768], P(None, 'dp'), may hold values from -6 to 6
- cotangent: bfloat16 [2, 16, 256, 768], P(None, 'dp'), may hold values from -6 to 6
- lengths: int32 [2, 16], P(None, 'dp'), may hold values from 64 to 256, as said below
- w_query: bfloat16 [2, 768, 768], P('section'), may hold values from -0.21875 to 0.21875
- w_key: bfloat16 [2, 768, 768], P('section'), may hold values from -0.21875 to 0.21875
- w_value: bfloat16 [2, 768, 768], P('section'), may hold values from -0.21875 to 0.21875
- w_output: bfloat16 [2, 768, 768], P('section'), may hold values from -1.75 to 1.75
- w_in: bfloat16 [2, 768, 3072], P('section'), may hold values from -0.21875 to 0.21875
- w_out: bfloat16 [2, 3072, 768], P('section'), may hold values from -0.109375 to 0.109375
- gain_attn: float32 [2, 768], P('section'), may hold values from 0.5 to 1.5
- gain_ffn: float32 [2, 768], P('section'), may hold values from 0.5 to 1.5
- mix_pre: float32 [2, 12, 12], P('section'), may hold values from -1.75 to 1.75
- mix_post: float32 [2, 12, 12], P('section'), may hold values from -1.75 to 1.75
Outputs:
- layer_outputs: bfloat16 [2, 2, 16, 256, 768], P('section', None, 'dp')
- input_grads: bfloat16 [2, 2, 16, 256, 768], P('section', None, 'dp')
- grad_query: float32 [2, 768, 768], P('section')
- grad_key: float32 [2, 768, 768], P('section')
- grad_value: float32 [2, 768, 768], P('section')
- grad_output: float32 [2, 768, 768], P('section')
- grad_in: float32 [2, 768, 3072], P('section')
- grad_out: float32 [2, 3072, 768], P('section')
- grad_gain_attn: float32 [2, 768], P('section')
- grad_gain_ffn: float32 [2, 768], P('section')
- grad_mix_pre: float32 [2, 12, 12], P('section')
- grad_mix_post: float32 [2, 12, 12], P('section')
- rms_stats: float32 [2, 3], P('section')
Inputs may be any that keep to these rules, and one draw needn't show every extreme that they name: Sequence s of micro-batch m holds valid tokens at positions 0 to lengths[m, s] - 1 of its padded row; some sequence has length 256 and some has length 64.
All inputs are finite; a program needn't handle non-finite values.
Results may differ from a plain program's by a relative error of at most 0.018.
Values may be sent and summed in bfloat16 or wider, within the bound.
No kernel may reach another device: no remote copies, remote signals or barrier semaphores. Data moves between devices by JAX's collectives and lax.ppermute only.
A program may use at most 256 MiB of HBM per device.

v0:
```python
import jax
import jax.numpy as jnp
from jax import lax
from jax.sharding import PartitionSpec as P

EPSILON = 1e-06
MASKED = -1e30
F32 = jnp.float32
BF16 = jnp.bfloat16


def dot(a, b, dims):
    return lax.dot_general(a, b, ((dims[0], dims[1]), ((), ())), preferred_element_type=F32)


def mix_heads(mix, values):
    return jnp.einsum("gh,hij->gij", mix, values, precision=lax.Precision.HIGH)


def norm_scale(values):
    return lax.rsqrt(jnp.mean(values * values, axis=-1, keepdims=True) + EPSILON)


def norm_back(values, gain, grad):
    scale = norm_scale(values)
    weighted = grad * gain
    inner = jnp.mean(values * weighted, axis=-1, keepdims=True)
    grad_values = scale * weighted - values * (scale * scale * scale) * inner
    grad_gain = jnp.sum(grad * values * scale, axis=0)
    return (grad_values, grad_gain)


def gelu_pair(values):
    inner = 0.7978845608028654 * (values + 0.044715 * values * values * values)
    tanh = jnp.tanh(inner)
    value = 0.5 * values * (1.0 + tanh)
    slope = 0.5 * (1.0 + tanh) + 0.5 * values * (1.0 - tanh * tanh) * (
        0.7978845608028654 * (1.0 + 3.0 * 0.044715 * values * values)
    )
    return (value, slope)


def forward(values, valid, params):
    w_query, w_key, w_value, w_output, w_in, w_out, gain_attn, gain_ffn, mix_pre, mix_post = params
    length, width = values.shape
    heads = mix_pre.shape[0]
    split = (length, heads, width // heads)
    normed = (values * norm_scale(values) * gain_attn).astype(BF16)
    query = dot(normed, w_query, ((1,), (0,))).astype(BF16).reshape(split)
    key = dot(normed, w_key, ((1,), (0,))).astype(BF16).reshape(split)
    value = dot(normed, w_value, ((1,), (0,))).astype(BF16).reshape(split)
    scores = jnp.einsum("ihd,jhd->hij", query, key, preferred_element_type=F32) * split[2] ** (-0.5)
    rows = lax.broadcasted_iota(jnp.int32, (length, length), 0)
    columns = lax.broadcasted_iota(jnp.int32, (length, length), 1)
    logits = jnp.where(columns <= rows, mix_heads(mix_pre, scores), MASKED)
    exponent = jnp.exp(logits - jnp.max(logits, axis=-1, keepdims=True))
    probs = exponent / jnp.sum(exponent, axis=-1, keepdims=True)
    weights = mix_heads(mix_post, probs).astype(BF16)
    head_out = jnp.einsum("hij,jhd->ihd", weights, value, preferred_element_type=F32)
    head_out = head_out.astype(BF16).reshape(length, width)
    branch_attn = dot(head_out, w_output, ((1,), (0,)))
    residual = values + branch_attn
    normed_ffn = (residual * norm_scale(residual) * gain_ffn).astype(BF16)
    pre_act = dot(normed_ffn, w_in, ((1,), (0,)))
    activation, slope = gelu_pair(pre_act)
    activation = activation.astype(BF16)
    branch_ffn = dot(activation, w_out, ((1,), (0,)))
    out = valid * (residual + branch_ffn)
    squares = jnp.stack(
        [
            jnp.sum(jnp.mean(out * out, axis=-1)),
            jnp.sum(valid[:, 0] * jnp.mean(branch_attn * branch_attn, axis=-1)),
            jnp.sum(valid[:, 0] * jnp.mean(branch_ffn * branch_ffn, axis=-1)),
        ]
    )
    saved = (
        normed,
        query,
        key,
        value,
        scores,
        probs,
        weights,
        head_out,
        residual,
        normed_ffn,
        activation,
        slope,
    )
    return (out.astype(BF16), squares, saved)


def backward_ffn(grad_sum, params, saved):
    w_in, w_out, gain_ffn = (params[4], params[5], params[7])
    residual, normed_ffn, activation, slope = saved[8:]
    grad_branch = grad_sum.astype(BF16)
    grad_act = dot(grad_branch, w_out, ((1,), (1,)))
    grad_pre = (grad_act * slope).astype(BF16)
    grad_normed = dot(grad_pre, w_in, ((1,), (1,)))
    back, grad_gain = norm_back(residual, gain_ffn, grad_normed)
    return (grad_sum + back, grad_gain, (activation, grad_branch, normed_ffn, grad_pre))


def backward_attention(values, grad_resid, params, saved):
    w_query, w_key, w_value, w_output = params[:4]
    gain_attn, mix_pre, mix_post = (params[6], params[8], params[9])
    normed, query, key, value, scores, probs, weights, head_out = saved[:8]
    length, heads, size = query.shape
    grad_attn = grad_resid.astype(BF16)
    grad_heads = dot(grad_attn, w_output, ((1,), (1,))).astype(BF16).reshape(query.shape)
    grad_weights = jnp.einsum("ihd,jhd->hij", grad_heads, value, preferred_element_type=F32)
    grad_value = jnp.einsum("hij,ihd->jhd", weights, grad_heads, preferred_element_type=F32)
    grad_mix_post = jnp.einsum("gij,hij->gh", grad_weights, probs, precision=lax.Precision.HIGH)
    grad_probs = mix_heads(mix_post.T, grad_weights)
    grad_logits = probs * (grad_probs - jnp.sum(probs * grad_probs, axis=-1, keepdims=True))
    grad_mix_pre = jnp.einsum("gij,hij->gh", grad_logits, scores, precision=lax.Precision.HIGH)
    grad_scores = mix_heads(mix_pre.T, grad_logits).astype(BF16)
    scale = size ** (-0.5)
    grad_query = jnp.einsum("hij,jhd->ihd", grad_scores, key, preferred_element_type=F32) * scale
    grad_key = jnp.einsum("hij,ihd->jhd", grad_scores, query, preferred_element_type=F32) * scale
    width = heads * size
    pieces = tuple(
        (piece.astype(BF16).reshape(length, width) for piece in (grad_query, grad_key, grad_value))
    )
    grad_normed = sum(
        (
            dot(piece, matrix, ((1,), (1,)))
            for piece, matrix in zip(pieces, (w_query, w_key, w_value))
        )
    )
    back, grad_gain = norm_back(values, gain_attn, grad_normed)
    return (
        grad_resid + back,
        grad_gain,
        grad_mix_pre,
        grad_mix_post,
        (normed, head_out, grad_attn) + pieces,
    )


def local(
    inputs,
    cotangent,
    lengths,
    w_query,
    w_key,
    w_value,
    w_output,
    w_in,
    w_out,
    gain_attn,
    gain_ffn,
    mix_pre,
    mix_post,
):
    core = lax.axis_index("section")
    is_first = core == 0
    swap = lambda shard: lax.ppermute(shard, "section", [(0, 1), (1, 0)])
    length, width = inputs.shape[2:]
    hidden = w_in.shape[2]
    own = (w_query, w_key, w_value, w_output, w_in, w_out, gain_attn, gain_ffn, mix_pre, mix_post)
    other = tuple((swap(weight) for weight in own))
    layers = (
        tuple((jnp.where(is_first, a, b)[0] for a, b in zip(own, other))),
        tuple((jnp.where(is_first, b, a)[0] for a, b in zip(own, other))),
    )
    take = lambda whole: lax.dynamic_index_in_dim(whole, core, 0, keepdims=False)[0]
    values = take(inputs).astype(F32)
    upstream = take(cotangent).astype(F32)
    valid = (lax.broadcasted_iota(jnp.int32, (length, 1), 0) < take(lengths)).astype(F32)
    outputs, squares, kept, starts = ([], [], [], [])
    layer_in = values
    for params in layers:
        starts.append(layer_in)
        rounded, square, saved = forward(layer_in, valid, params)
        outputs.append(rounded)
        squares.append(square)
        kept.append(saved)
        layer_in = rounded.astype(F32)

    def split_cols(array):
        half = array.shape[1] // 2
        mine = lax.dynamic_slice_in_dim(array, core * half, half, 1)
        theirs = lax.dynamic_slice_in_dim(array, (1 - core) * half, half, 1)
        return (mine, theirs)

    def both_rows(array):
        return jnp.concatenate([array, swap(array)], axis=0)

    def both_half(array):
        mine, theirs = split_cols(array)
        return jnp.concatenate([mine, swap(theirs)], axis=0)

    def weight_grad(left, right):
        return dot(left, right, ((0,), (0,))).astype(BF16)

    grads = [None, None]
    small = [None, None]
    input_grads = [None, None]
    for index in (1, 0):
        params, saved = (layers[index], kept[index])
        grad_sum = valid * upstream
        grad_resid, gain_ffn_grad, ffn = backward_ffn(grad_sum, params, saved)
        activation, grad_branch, normed_ffn, grad_pre = ffn
        down = weight_grad(both_half(activation), both_rows(grad_branch))
        up = weight_grad(both_rows(normed_ffn), both_half(grad_pre))
        grad_in, gain_attn_grad, mix_pre_grad, mix_post_grad, attn = backward_attention(
            starts[index], grad_resid, params, saved
        )
        normed, head_out, grad_attn, grad_query, grad_key, grad_value = attn
        rows = both_rows(normed)
        sides = [
            weight_grad(rows, both_half(piece)) for piece in (grad_query, grad_key, grad_value)
        ]
        sides.append(weight_grad(both_rows(head_out), both_half(grad_attn)))
        blocks = [down]
        blocks += [up[:, at * width : (at + 1) * width] for at in range(up.shape[1] // width)]
        blocks += [jnp.concatenate(sides[:2], axis=1), jnp.concatenate(sides[2:], axis=1)]
        grads[index] = jnp.concatenate(blocks, axis=0)
        small[index] = jnp.concatenate(
            [
                gain_attn_grad,
                gain_ffn_grad,
                mix_pre_grad.reshape(-1),
                mix_post_grad.reshape(-1),
                squares[index],
            ]
        )
        input_grads[index] = grad_in.astype(BF16)
        upstream = input_grads[index].astype(F32)
    shards = [lax.psum_scatter(grad, "dp", scatter_dimension=0, tiled=True) for grad in grads]
    mine = jnp.where(is_first, shards[0], shards[1])
    theirs = swap(jnp.where(is_first, shards[1], shards[0]))
    halves = jnp.concatenate(
        [jnp.where(is_first, mine, theirs), jnp.where(is_first, theirs, mine)], axis=0
    )
    whole = lax.all_gather(halves, "dp", axis=0)
    ranks = whole.shape[0]
    whole = (
        whole.reshape(ranks, 2, -1, width).transpose(1, 0, 2, 3).reshape(2, -1, width).astype(F32)
    )
    half = width // 2
    count = hidden // 2
    w_out_grad = whole[:, :count].reshape(1, hidden, width)
    blocks = hidden // 2 // width
    up = whole[:, count : count + blocks * width].reshape(2 * blocks, width, width)
    w_in_grad = up.transpose(1, 0, 2).reshape(1, width, hidden)
    rest = whole[:, count + blocks * width :].reshape(2, 2, width, 2, half)
    rest = rest.transpose(1, 3, 2, 0, 4).reshape(4, 1, width, width)
    both = jnp.stack(small)
    total_small = jnp.where(is_first, both, both[::-1])
    mine_small = total_small[0] + swap(total_small[1])
    tail = jnp.concatenate([mine_small, jnp.sum(valid)[None] + swap(jnp.sum(valid)[None])])
    tail = lax.psum(tail, "dp")
    heads = mix_pre.shape[1]
    square = heads * heads
    at = 2 * width
    rms = jnp.sqrt(tail[at + 2 * square : at + 2 * square + 3] / tail[-1])[None]

    def place(pair):
        mine = jnp.where(is_first, pair[0], pair[1])
        theirs = swap(jnp.where(is_first, pair[1], pair[0]))
        ordered = [jnp.where(is_first, mine, theirs), jnp.where(is_first, theirs, mine)]
        return jnp.stack(ordered)[None, :, None]

    return (
        place(outputs),
        place(input_grads),
        rest[0],
        rest[1],
        rest[2],
        rest[3],
        w_in_grad,
        w_out_grad,
        tail[None, :width],
        tail[None, width:at],
        tail[at : at + square].reshape(1, heads, heads),
        tail[at + square : at + 2 * square].reshape(1, heads, heads),
        rms,
    )


def solution(mesh):
    in_specs = (
        P(None, "dp", None, None),
        P(None, "dp", None, None),
        P(None, "dp"),
        P("section", None, None),
        P("section", None, None),
        P("section", None, None),
        P("section", None, None),
        P("section", None, None),
        P("section", None, None),
        P("section", None),
        P("section", None),
        P("section", None, None),
        P("section", None, None),
    )
    out_specs = (
        P("section", None, "dp", None, None),
        P("section", None, "dp", None, None),
        P("section", None, None),
        P("section", None, None),
        P("section", None, None),
        P("section", None, None),
        P("section", None, None),
        P("section", None, None),
        P("section", None),
        P("section", None),
        P("section", None, None),
        P("section", None, None),
        P("section", None),
    )
    return jax.shard_map(local, mesh=mesh, in_specs=in_specs, out_specs=out_specs, check_vma=False)
```

profile of v0, /device:TPU:0, one launch (start us, length us, event | category | flops | bytes accessed | tf_op | source)
XLA Modules:
  0.0 790.0 jit_solution(18255932944527995268)
XLA Ops:
  13.1 6.0 collective-permute-done.2
  28.9 3.0 convolution_convert_fusion.22
  33.2 1.9 copy.157
  36.4 1.8 convolution_multiply_fusion.1
  38.2 4.2 select_reduce_fusion.1
  42.4 2.1 copy-done.4
  44.5 1.9 fusion.45
  47.4 4.8 fusion.204
  54.6 2.3 multiply_reduce_fusion.13
  57.7 6.3 multiply_convert_fusion.1
  64.0 2.5 fusion.138
  69.3 1.8 convolution_convert_fusion.18
  72.0 1.8 convolution_convert_fusion.19
  74.8 1.8 convolution_multiply_fusion
  76.6 4.2 select_reduce_fusion
  80.8 2.2 fusion.47
  83.0 3.1 fusion.199
  86.9 2.7 multiply_reduce_fusion.12
  89.9 4.2 multiply_convert_fusion
  94.2 5.9 fusion.38
  100.0 5.2 multiply_reduce_fusion.5
  105.3 5.8 fusion.246
  111.8 2.6 convolution_convert_fusion.15
  114.4 1.9 copy.166
  116.4 2.5 convolution_convert_fusion.14
  118.9 1.9 fusion.253
  120.8 6.9 multiply_reduce_fusion.1
  127.8 4.3 fusion.74
  133.5 2.1 fusion.90
  139.6 3.1 fusion.41
  144.7 2.5 multiply_reduce_fusion.6
  150.5 1.9 copy.171
  152.4 2.5 convolution_convert_fusion.12
  154.9 1.7 fusion.254
  156.7 6.7 multiply_reduce_fusion
  163.5 4.3 fusion.75
  171.4 2.1 fusion.131
  176.8 1.7 convolution_convert_fusion.8
  182.6 2.8 fusion.49
  203.0 2.8 fusion.48
  210.3 132.8 %reduce-scatter.3.cloned.1.call-done = bf16[288,768]{1,0:T(8,128)(2,1)} async-done(((bf16[4608,768]{1,0:T(8,128)(2,1)}), bf16[288,768]{1,0:T(8,128)(2,1)}) %reduce-scatter.3.cloned.1.call-update) | async-done | bytes 442384 | tf_op jit(solution)/shard_map/reduce_scatter | solution.py:231
  343.1 155.2 %reduce-scatter.5.cloned.1.call-done = bf16[288,768]{1,0:T(8,128)(2,1)} async-done(((bf16[4608,768]{1,0:T(8,128)(2,1)}), bf16[288,768]{1,0:T(8,128)(2,1)}) %reduce-scatter.5.cloned.1.call-update) | async-done | bytes 442384 | tf_op jit(solution)/shard_map/reduce_scatter | solution.py:231
  499.4 1.8 collective-permute-done.32
  508.5 1.8 broadcast_select_fusion.42
  510.3 9.0 %fusion.104 = f32[12,12]{1,0:T(8,128)} fusion(f32[12,256,256]{2,1,0:T(8,128)} %copy-done.30, f32[12,256,256]{2,0,1:T(8,128)} %copy-done.6, f32[12,256]{0,1:T(8,128)} %copy-done.83, f32[12,256]{0,1:T(8,128)} %copy-done.68, pred[256,256]{1,0:T(8,128)(4,1)} %iota_compare_fusion), kind=kOutput, calls=%fused_computation.176 | convolution fusion | flops 58982400 | bytes 6382144 | tf_op jit(solution)/shard_map/gij,hij->gh/dot_general | solution.py:113
  520.6 10.1 %fusion.113 = f32[12,12]{1,0:T(8,128)} fusion(f32[12,256,256]{2,1,0:T(8,128)S(1)} %convolution_multiply_fusion, f32[12,256,256]{2,0,1:T(8,128)} %copy-done.118, f32[12,256]{0,1:T(8,128)} %copy-done.120, f32[12,256,256]{2,0,1:T(8,128)} %copy-done.6, f32[12,256]{0,1:T(8,128)} %copy-done.83, f32[12,256]{0,1:T(8,128)} %copy-done.68, ...), kind=kOutput, calls=%fused_computation.179 | convolution fusion | flops 60555264 | bytes 9540160 | tf_op jit(solution)/shard_map/gij,hij->gh/dot_general | solution.py:116
  532.7 1.9 select_reduce_fusion.3
  534.6 1.9 select_reduce_fusion.2
  536.5 2.7 concatenate.118
  539.2 8.8 %fusion.107 = f32[12,12]{1,0:T(8,128)} fusion(f32[12,256,256]{2,1,0:T(8,128)} %copy-done.31, f32[12,256,256]{2,0,1:T(8,128)} %copy-done.4, f32[12,256]{0,1:T(8,128)} %copy-done.81, f32[12,256]{0,1:T(8,128)} %copy-done.66, pred[256,256]{1,0:T(8,128)(4,1)} %iota_compare_fusion), kind=kOutput, calls=%fused_computation.177 | convolution fusion | flops 58982400 | bytes 6382144 | tf_op jit(solution)/shard_map/gij,hij->gh/dot_general | solution.py:113
  549.3 9.7 %fusion.110 = f32[12,12]{1,0:T(8,128)} fusion(f32[12,256,256]{2,1,0:T(8,128)S(1)} %copy-done.3, f32[12,256,256]{2,0,1:T(8,128)} %copy-done.119, f32[12,256]{0,1:T(8,128)} %copy-done.121, f32[12,256,256]{2,0,1:T(8,128)} %copy-done.4, f32[12,256]{0,1:T(8,128)} %copy-done.81, f32[12,256]{0,1:T(8,128)} %copy-done.66, pred[256,256]{1,0:T(8,128)(4,1)} %iota_compare_fusion), kind=kOutput, calls=%fused_computation.178 | convolution fusion | flops 60555264 | bytes 9540160 | tf_op jit(solution)/shard_map/gij,hij->gh/dot_general | solution.py:116
  561.1 1.9 select_reduce_fusion.4
  563.0 2.7 concatenate.117
  567.4 2.1 broadcast_select_fusion.40
  569.7 42.1 %psum.7 = f32[1828]{0:T(1024)S(1)} all-reduce(f32[1828]{0:T(1024)S(1)} %pad_maximum_fusion.10), channel_id=1, replica_groups=mesh['section'=2,'dp'=16] {'dp'}, use_global_device_ids=true, to_apply=%region_33.34 | all-reduce | flops 1828 | bytes 14624 | tf_op jit(solution)/shard_map/psum | solution.py:254
  619.4 51.2 %all-gather.3.cloned.1.call-done = bf16[9216,768]{1,0:T(8,128)(2,1)} async-done(((bf16[576,768]{1,0:T(8,128)(2,1)}), bf16[9216,768]{1,0:T(8,128)(2,1)}) %all-gather.3.cloned.1.call-update) | async-done | bytes 14155792 | tf_op jit(solution)/shard_map/all_gather | solution.py:237
  670.6 15.8 %copy.184 = f32[16,2,288,768]{3,2,0,1:T(8,128)} copy(bf16[16,2,288,768]{3,2,1,0:T(8,128)(2,1)} %bitcast.301) | data formatting | bytes 42467328 | tf_op jit(solution)/shard_map/convert_element_type | solution.py:240
  686.4 20.8 %fusion.250 = (f32[2,1536,768]{2,1,0:T(8,128)}, f32[2,1536,768]{2,1,0:T(8,128)}, f32[2,1536,768]{2,1,0:T(8,128)}) fusion(f32[2,4608,768]{2,1,0:T(8,128)} %bitcast.298), kind=kLoop, calls=%fused_computation.396 | loop fusion | bytes 56623104 | tf_op jit(solution)/shard_map/slice | solution.py:244
  707.1 13.4 %copy.186 = f32[768,4,768]{2,1,0:T(4,128)} copy(f32[768,4,768]{2,0,1:T(8,128)} %bitcast.299) | data formatting | bytes 18874368 | tf_op jit(solution)/shard_map/transpose | solution.py:247
  720.6 12.3 %reshape.281 = f32[1,768,3072]{2,1,0:T(8,128)} reshape(f32[768,4,768]{2,1,0:T(4,128)} %copy.186) | data formatting | bytes 18874368 | tf_op jit(solution)/shard_map/reshape | solution.py:247
  732.8 12.4 %reshape.278 = f32[2,2,768,2,384]{4,3,2,1,0:T(2,128)} reshape(f32[2,1536,768]{2,1,0:T(8,128)} %get-tuple-element.101) | data formatting | bytes 18874368 | tf_op jit(solution)/shard_map/reshape | solution.py:248
  745.3 17.1 %copy.185 = f32[2,2,768,2,384]{4,3,2,1,0:T(2,128)} copy(f32[2,2,768,2,384]{4,1,2,0,3:T(2,128)} %bitcast.300) | data formatting | bytes 18874368 | tf_op jit(solution)/shard_map/transpose | solution.py:249
  762.4 13.2 %reshape.279 = f32[4,1,768,768]{3,2,1,0:T(8,128)} reshape(f32[2,2,768,2,384]{4,3,2,1,0:T(2,128)} %copy.185) | data formatting | bytes 18874368 | tf_op jit(solution)/shard_map/reshape | solution.py:249
  775.6 7.6 slice_bitcast_fusion
  (445 shorter events, 94.6 us)
Async XLA Ops:
  7.2 24.7 %copy-start.15 = (bf16[1,768,768]{2,1,0:T(8,128)(2,1)S(1)}, bf16[1,768,768]{2,1,0:T(8,128)(2,1)}, u32[]{:S(2)}) copy-start(bf16[1,768,768]{2,1,0:T(8,128)(2,1)} %param.17) | copy-start | bytes 3538948
  7.2 335.9 %reduce-scatter.3.cloned.1.call-start = ((), (), s32[]{:S(2)}) async-start(), calls=%async_computation.2 | async-start | bytes 7520256 | tf_op jit(solution)/shard_map/reduce_scatter | solution.py:231
  7.3 21.5 %collective-permute-start.4 = (bf16[1,768,768]{2,1,0:T(8,128)(2,1)}, bf16[1,768,768]{2,1,0:T(8,128)(2,1)S(1)}, u32[]{:S(2)}, u32[]{:S(2)}) collective-permute-start(bf16[1,768,768]{2,1,0:T(8,128)(2,1)} %param.16), channel_id=1, source_target_pairs={{0,16},{16,0},{1,17},{17,1},{2,18},{18,2},{3,19},{19,3},{4,20},{20... | collective-permute-start | bytes 3538952 | tf_op jit(solution)/shard_map/ppermute | solution.py:158
  7.8 49.9 %collective-permute-start.8 = (bf16[1,768,3072]{2,1,0:T(8,128)(2,1)}, bf16[1,768,3072]{2,1,0:T(8,128)(2,1)}, u32[]{:S(2)}, u32[]{:S(2)}) collective-permute-start(bf16[1,768,3072]{2,1,0:T(8,128)(2,1)} %param.20), channel_id=1, source_target_pairs={{0,16},{16,0},{1,17},{17,1},{2,18},{18,2},{3,19},{19,3},{4,20},{20... | collective-permute-start | bytes 14155784 | tf_op jit(solution)/shard_map/ppermute | solution.py:158
  7.9 5.2 collective-permute-start.3
  8.3 10.8 %collective-permute-start.2 = (f32[1,12,12]{2,0,1:T(1,128)}, f32[1,12,12]{2,0,1:T(1,128)}, u32[]{:S(2)}, u32[]{:S(2)}) collective-permute-start(f32[1,12,12]{2,0,1:T(1,128)} %param.25), channel_id=1, source_target_pairs={{0,16},{16,0},{1,17},{17,1},{2,18},{18,2},{3,19},{19,3},{4,20},{20... | collective-permute-start | bytes 1736 | tf_op jit(solution)/shard_map/ppermute | solution.py:158
  8.4 23.5 %collective-permute-start.5 = (bf16[1,768,768]{2,1,0:T(8,128)(2,1)}, bf16[1,768,768]{2,1,0:T(8,128)(2,1)S(1)}, u32[]{:S(2)}, u32[]{:S(2)}) collective-permute-start(bf16[1,768,768]{2,1,0:T(8,128)(2,1)} %param.17), channel_id=1, source_target_pairs={{0,16},{16,0},{1,17},{17,1},{2,18},{18,2},{3,19},{19,3},{4,20},{20... | collective-permute-start | bytes 3538952 | tf_op jit(solution)/shard_map/ppermute | solution.py:158
  13.0 12.6 %collective-permute-start = (f32[1,768]{1,0:T(1,128)}, f32[1,768]{1,0:T(1,128)S(1)}, u32[]{:S(2)}, u32[]{:S(2)}) collective-permute-start(f32[1,768]{1,0:T(1,128)} %param.22), channel_id=1, source_target_pairs={{0,16},{16,0},{1,17},{17,1},{2,18},{18,2},{3,19},{19,3},{4,20},{20... | collective-permute-start | bytes 9224 | tf_op jit(solution)/shard_map/ppermute | solution.py:158
  19.0 8.0 %collective-permute-start.7 = (f32[1,768]{1,0:T(1,128)}, f32[1,768]{1,0:T(1,128)}, u32[]{:S(2)}, u32[]{:S(2)}) collective-permute-start(f32[1,768]{1,0:T(1,128)} %param.23), channel_id=1, source_target_pairs={{0,16},{16,0},{1,17},{17,1},{2,18},{18,2},{3,19},{19,3},{4,20},{20... | collective-permute-start | bytes 9224 | tf_op jit(solution)/shard_map/ppermute | solution.py:158
  25.6 6.3 copy-start.93
  26.1 20.3 %collective-permute-start.1 = (bf16[1,768,768]{2,1,0:T(8,128)(2,1)}, bf16[1,768,768]{2,1,0:T(8,128)(2,1)}, u32[]{:S(2)}, u32[]{:S(2)}) collective-permute-start(bf16[1,768,768]{2,1,0:T(8,128)(2,1)} %param.18), channel_id=1, source_target_pairs={{0,16},{16,0},{1,17},{17,1},{2,18},{18,2},{3,19},{19,3},{4,20},{20... | collective-permute-start | bytes 3538952 | tf_op jit(solution)/shard_map/ppermute | solution.py:158
  27.0 37.0 %collective-permute-start.9 = (bf16[1,3072,768]{2,1,0:T(8,128)(2,1)}, bf16[1,3072,768]{2,1,0:T(8,128)(2,1)}, u32[]{:S(2)}, u32[]{:S(2)}) collective-permute-start(bf16[1,3072,768]{2,1,0:T(8,128)(2,1)} %param.21), channel_id=1, source_target_pairs={{0,16},{16,0},{1,17},{17,1},{2,18},{18,2},{3,19},{19,3},{4,20},{20... | collective-permute-start | bytes 14155784 | tf_op jit(solution)/shard_map/ppermute | solution.py:158
  28.8 25.8 %collective-permute-start.6 = (bf16[1,768,768]{2,1,0:T(8,128)(2,1)}, bf16[1,768,768]{2,1,0:T(8,128)(2,1)}, u32[]{:S(2)}, u32[]{:S(2)}) collective-permute-start(bf16[1,768,768]{2,1,0:T(8,128)(2,1)} %param.19), channel_id=1, source_target_pairs={{0,16},{16,0},{1,17},{17,1},{2,18},{18,2},{3,19},{19,3},{4,20},{20... | collective-permute-start | bytes 3538952 | tf_op jit(solution)/shard_map/ppermute | solution.py:158
  47.4 7.2 copy-start.36
  47.4 7.2 copy-start.111
  53.6 121.6 %collective-permute-start.20 = (bf16[256,768]{0,1:T(8,128)(2,1)}, bf16[256,768]{0,1:T(8,128)(2,1)}, u32[]{:S(2)}, u32[]{:S(2)}) collective-permute-start(bf16[256,768]{0,1:T(8,128)(2,1)} %bitcast.10), channel_id=1, source_target_pairs={{0,16},{16,0},{1,17},{17,1},{2,18},{18,2},{3,19},{19,3},{4,20},{20... | collective-permute-start | bytes 1179656 | tf_op jit(solution)/shard_map/ppermute | solution.py:158
  56.9 7.1 copy-start.32
  57.5 6.5 copy-start.96
  57.5 6.5 slice-start
  57.6 6.4 copy-start.103
  57.6 6.4 slice-start.1
  80.8 9.0 %slice-start.6 = ((s8[4718592]{0:T(1024)(128)(4,1)}), s8[4194304]{0:T(1024)(128)(4,1)S(1)}, s32[]{:S(2)}) async-start(s8[4718592]{0:T(1024)(128)(4,1)} %bitcast.340), calls=%async_computation.11 | async-start | bytes 8388608
  83.0 6.8 slice-start.7
  86.9 7.2 slice-start.2
  94.1 11.1 %copy-start.44 = (bf16[256,3072]{1,0:T(8,128)(2,1)}, bf16[256,3072]{1,0:T(8,128)(2,1)S(1)}, u32[]{:S(2)}) copy-start(bf16[256,3072]{1,0:T(8,128)(2,1)S(1)} %get-tuple-element.167) | copy-start | bytes 4718596
  118.8 14.6 %copy-start.27 = (bf16[12,64,256]{2,1,0:T(8,128)(2,1)}, bf16[12,64,256]{2,1,0:T(8,128)(2,1)S(1)}, u32[]{:S(2)}) copy-start(bf16[12,64,256]{2,1,0:T(8,128)(2,1)S(1)} %convolution_convert_fusion.14) | copy-start | bytes 1179652
  120.8 6.9 copy-start.30
  120.8 7.0 copy-start.100
  137.6 6.4 slice-start.8
  139.2 7.9 %copy-start.8 = (bf16[256,768]{1,0:T(8,128)(2,1)}, bf16[256,768]{1,0:T(8,128)(2,1)S(1)}, u32[]{:S(2)}) copy-start(bf16[256,768]{1,0:T(8,128)(2,1)S(1)} %get-tuple-element.90) | copy-start | bytes 1179652
  156.7 6.7 copy-start.31
  156.7 6.8 copy-start.98
  169.2 11.9 %collective-permute-start.15 = (bf16[256,1536]{1,0:T(8,128)(2,1)S(1)}, bf16[256,1536]{1,0:T(8,128)(2,1)S(1)}, u32[]{:S(2)}, u32[]{:S(2)}) collective-permute-start(bf16[256,1536]{1,0:T(8,128)(2,1)S(1)} %copy-done.64), channel_id=1, source_target_pairs={{0,16},{16,0},{1,17},{17,1},{2,18},{18,2},{3,19},{19,3},{4,20},{20... | collective-permute-start | bytes 2359304 | tf_op jit(solution)/shard_map/ppermute | solution.py:158
  173.5 5.0 collective-permute-start.16
  174.7 1.5 collective-permute-start.21
  174.7 1.8 collective-permute-start.18
  175.3 7.3 collective-permute-start.12
  176.2 4.9 collective-permute-start.14
  176.6 2.9 collective-permute-start.19
  178.6 1.9 collective-permute-start.17
  179.5 3.1 collective-permute-start.13
  189.8 308.4 %reduce-scatter.5.cloned.1.call-start = ((), (), s32[]{:S(2)}) async-start(), calls=%async_computation.3 | async-start | bytes 7520256 | tf_op jit(solution)/shard_map/reduce_scatter | solution.py:231
  190.1 7.7 collective-permute-start.26
  191.7 4.0 collective-permute-start.31
  193.1 2.9 collective-permute-start.29
  194.9 6.7 collective-permute-start.25
  195.3 2.2 collective-permute-start.28
  195.7 5.3 collective-permute-start.30
  196.0 7.0 collective-permute-start.22
  197.5 4.0 collective-permute-start.24
  197.8 2.2 collective-permute-start.27
  200.0 3.0 collective-permute-start.23
  210.3 297.0 %copy-start.110 = (f32[256]{0:T(256)S(1)}, f32[256]{0:T(256)}, u32[]{:S(2)}) copy-start(f32[256]{0:T(256)} %get-tuple-element.125) | copy-start | bytes 3076
  210.3 460.3 %all-gather.3.cloned.1.call-start = ((), (), s32[]{:S(2)}) async-start(), calls=%async_computation.4 | async-start | bytes 15040512 | tf_op jit(solution)/shard_map/all_gather | solution.py:237
  499.4 1.9 collective-permute-start.32
  504.6 1.4 collective-permute-start.34
  510.3 105.9 %collective-permute-start.10 = (bf16[256,768]{1,0:T(8,128)(2,1)}, bf16[256,768]{1,0:T(8,128)(2,1)}, u32[]{:S(2)}, u32[]{:S(2)}) collective-permute-start(bf16[256,768]{1,0:T(8,128)(2,1)} %broadcast_select_fusion.42), channel_id=1, source_target_pairs={{0,16},{16,0},{1,17},{17,1},{2,18},{18,2},{3,19},{19,3},{4,20},{20... | collective-permute-start | bytes 1179656 | tf_op jit(solution)/shard_map/ppermute | solution.py:158
  520.6 15.8 %copy-start.108 = (f32[768]{0:T(1024)S(1)}, f32[768]{0:T(1024)}, u32[]{:S(2)}) copy-start(f32[768]{0:T(1024)} %get-tuple-element.69) | copy-start | bytes 9220
  539.2 10.1 %copy-start.3 = (f32[12,256,256]{2,1,0:T(8,128)S(1)}, f32[12,256,256]{2,1,0:T(8,128)}, u32[]{:S(2)}) copy-start(f32[12,256,256]{2,1,0:T(8,128)} %copy-done.2) | copy-start | bytes 9437188
  559.0 57.3 %copy-start.51 = (bf16[256,768]{1,0:T(8,128)(2,1)S(1)}, bf16[256,768]{1,0:T(8,128)(2,1)}, u32[]{:S(2)}) copy-start(bf16[256,768]{1,0:T(8,128)(2,1)} %get-tuple-element.123) | copy-start | bytes 1179652
  566.2 3.3 collective-permute-start.33
  567.4 51.0 %copy-start.9 = (bf16[256,768]{1,0:T(8,128)(2,1)S(1)}, bf16[256,768]{1,0:T(8,128)(2,1)}, u32[]{:S(2)}) copy-start(bf16[256,768]{1,0:T(8,128)(2,1)} %copy-done.8) | copy-start | bytes 1179652
  569.5 48.8 %collective-permute-start.11 = (bf16[256,768]{1,0:T(8,128)(2,1)S(1)}, bf16[256,768]{1,0:T(8,128)(2,1)S(1)}, u32[]{:S(2)}, u32[]{:S(2)}) collective-permute-start(bf16[256,768]{1,0:T(8,128)(2,1)S(1)} %get-tuple-element.85), channel_id=1, source_target_pairs={{0,16},{16,0},{1,17},{17,1},{2,18},{18,2},{3,19},{19,3},{4,20},{20... | collective-permute-start | bytes 1179656 | tf_op jit(solution)/shard_map/ppermute | solution.py:158
  775.6 7.6 copy-start.1
  (106 other events, 358.9 us)
Sparse Core Ops, SparseCore 0:
  190.0 153.1 reduce-scatter.2
  349.0 149.2 reduce-scatter.4
  503.5 167.0 all-gather.2
where the time goes:
time: 800 us; the launch traced here: 790 us
  waiting for transfers between devices  351 us (44%)
  matrix products  167 us (21%)
  local copies, waits for them, and re-layouts  160 us (20%)
  blocking collectives  42.1 us (5%)
  other arithmetic  41.5 us (5%)
  between operations  17.4 us (2%)
  starting transfers between devices  10.8 us (1%)
    reduce_scatter x2, waiting for transfers between devices, local(): lax.psum_scatter(grad, 'dp', scatter_dimension=0, tiled=True)  288 us
    dot_general x36, matrix products, dot(): lax.dot_general(a, b, ((dims[0], dims[1]), ((), ())), preferred_element_t...  74.7 us
    all_gather x1, waiting for transfers between devices, local(): whole = lax.all_gather(halves, 'dp', axis=0)  51.2 us
    psum x1, blocking collectives, local(): tail = lax.psum(tail, 'dp')  42.1 us
    dot_general x8, matrix products, mix_heads(): return jnp.einsum('gh,hij->gij', mix, values, precision=lax.Precision.HIGH)  38.5 us
    slice x1, local copies, waits for them, and re-layouts, local(): w_out_grad = whole[:, :count].reshape(1, hidden, width)  20.8 us
    dot_general x2, matrix products, backward_attention(): jnp.einsum('gij,hij->gh', grad_logits, scores, precision=lax.Precision.HIGH)  19.8 us
    dot_general x2, matrix products, backward_attention(): jnp.einsum('gij,hij->gh', grad_weights, probs, precision=lax.Precision.HIGH)  17.7 us
  transfers between devices with their start and end apart: 38, of which 9 were waited for; matrix products, arithmetic and copies ran while one was open for 30% of the time, Pallas kernels for 0%

commit v1 on v0

--- a/solution.py
+++ b/solution.py
@@ -251,7 +251,7 @@
     total_small = jnp.where(is_first, both, both[::-1])
     mine_small = total_small[0] + swap(total_small[1])
     tail = jnp.concatenate([mine_small, jnp.sum(valid)[None] + swap(jnp.sum(valid)[None])])
-    tail = lax.psum(tail, "dp")
+    tail = jnp.sum(lax.all_gather(tail, "dp"), axis=0)
     heads = mix_pre.shape[1]
     square = heads * heads
     at = 2 * width

time: 800 us -> 910 us (1.14)
  waiting for transfers between devices: 351 us -> 498 us
  blocking collectives: 42.1 us -> 0 us
    all_gather x1, waiting for transfers between devices: 51.2 us -> 161 us  [local(): whole = lax.all_gather(halves, 'dp', axis=0)]
    unnamed x3 -> x5, waiting for transfers between devices: 0.05 us -> 97 us
    reduce_scatter x2, waiting for transfers between devices: 288 us -> 231 us  [local(): lax.psum_scatter(grad, 'dp', scatter_dimension=0, tiled=True)]
    psum x1 -> x0, blocking collectives: 42.1 us -> none  [local(): tail = lax.psum(tail, 'dp')]
  transfers between devices with their start and end apart: 38 -> 39, of which waited for: 9 -> 8; matrix products, arithmetic and copies ran while one was open for 30% -> 27% of each run, Pallas kernels for 0% -> 0%
where the time goes in v1:
time: 910 us; the launch traced here: 900 us
  waiting for transfers between devices  498 us (55%)
  matrix products  167 us (18%)
  local copies, waits for them, and re-layouts  163 us (18%)
  other arithmetic  42.8 us (5%)
  between operations  18.3 us (2%)
  starting transfers between devices  11.4 us (1%)
    reduce_scatter x2, waiting for transfers between devices, local(): lax.psum_scatter(grad, 'dp', scatter_dimension=0, tiled=True)  231 us
    all_gather x1, waiting for transfers between devices, local(): whole = lax.all_gather(halves, 'dp', axis=0)  161 us
    unnamed x5, waiting for transfers between devices  97 us
    dot_general x36, matrix products, dot(): lax.dot_general(a, b, ((dims[0], dims[1]), ((), ())), preferred_element_t...  74.7 us
    dot_general x8, matrix products, mix_heads(): return jnp.einsum('gh,hij->gij', mix, values, precision=lax.Precision.HIGH)  38.5 us
    slice x1, local copies, waits for them, and re-layouts, local(): w_out_grad = whole[:, :count].reshape(1, hidden, width)  20.8 us
    dot_general x2, matrix products, backward_attention(): jnp.einsum('gij,hij->gh', grad_logits, scores, precision=lax.Precision.HIGH)  19.5 us
  transfers between devices with their start and end apart: 39, of which 8 were waited for; matrix products, arithmetic and copies ran while one was open for 27% of the time, Pallas kernels for 0%

profile of v1, /device:TPU:0, one launch (start us, length us, event | category | flops | bytes accessed | tf_op | source)
XLA Modules:
  0.0 899.7 jit_solution(12333672199547816501)
XLA Ops:
  13.0 6.0 collective-permute-done.2
  28.9 3.0 convolution_convert_fusion.22
  33.2 1.9 copy.157
  36.3 1.8 convolution_multiply_fusion.1
  38.2 4.2 select_reduce_fusion.1
  42.4 2.1 copy-done.4
  44.5 1.9 fusion.45
  47.3 4.8 fusion.204
  54.6 2.3 multiply_reduce_fusion.13
  57.7 6.3 multiply_convert_fusion.1
  64.0 2.5 fusion.138
  69.3 1.8 convolution_convert_fusion.18
  72.0 1.8 convolution_convert_fusion.19
  74.8 1.8 convolution_multiply_fusion
  76.6 4.2 select_reduce_fusion
  80.8 2.4 fusion.47
  83.2 3.1 fusion.199
  87.1 2.8 multiply_reduce_fusion.12
  90.1 4.2 multiply_convert_fusion
  94.4 5.9 fusion.38
  100.3 5.2 multiply_reduce_fusion.5
  105.5 5.8 fusion.246
  112.0 2.6 convolution_convert_fusion.15
  114.7 1.9 copy.166
  116.6 2.5 convolution_convert_fusion.14
  119.1 1.9 fusion.253
  121.1 6.7 multiply_reduce_fusion.1
  127.8 4.3 fusion.74
  133.5 2.1 fusion.90
  139.6 3.1 fusion.41
  144.7 2.5 multiply_reduce_fusion.6
  150.5 1.9 copy.171
  152.5 2.5 convolution_convert_fusion.12
  154.9 1.7 fusion.254
  156.7 7.0 multiply_reduce_fusion
  163.7 4.3 fusion.75
  171.6 2.1 fusion.131
  177.1 1.7 convolution_convert_fusion.8
  182.8 2.8 fusion.49
  203.0 2.8 fusion.48
  212.2 8.6 fusion.104
  222.1 9.8 %fusion.113 = f32[12,12]{1,0:T(8,128)} fusion(f32[12,256,256]{2,1,0:T(8,128)S(1)} %convolution_multiply_fusion, f32[12,256,256]{2,0,1:T(8,128)} %copy-done.122, f32[12,256]{0,1:T(8,128)} %copy-done.124, f32[12,256,256]{2,0,1:T(8,128)} %copy-done.6, f32[12,256]{0,1:T(8,128)} %copy-done.86, f32[12,256]{0,1:T(8,128)} %copy-done.71, ...), kind=kOutput, calls=%fused_computation.179 | convolution fusion | flops 60555264 | bytes 9540160 | tf_op jit(solution)/shard_map/gij,hij->gh/dot_general | solution.py:116
  233.9 1.9 select_reduce_fusion.3
  235.8 1.9 select_reduce_fusion.2
  237.7 2.7 concatenate.118
  240.4 8.7 fusion.107
  250.5 9.7 %fusion.110 = f32[12,12]{1,0:T(8,128)} fusion(f32[12,256,256]{2,1,0:T(8,128)S(1)} %copy-done.3, f32[12,256,256]{2,0,1:T(8,128)} %copy-done.123, f32[12,256]{0,1:T(8,128)} %copy-done.125, f32[12,256,256]{2,0,1:T(8,128)} %copy-done.4, f32[12,256]{0,1:T(8,128)} %copy-done.84, f32[12,256]{0,1:T(8,128)} %copy-done.69, pred[256,256]{1,0:T(8,128)(4,1)} %iota_compare_fusion), kind=kOutput, calls=%fused_computation.178 | convolution fusion | flops 60555264 | bytes 9540160 | tf_op jit(solution)/shard_map/gij,hij->gh/dot_general | solution.py:116
  262.3 1.9 select_reduce_fusion.4
  264.2 2.7 concatenate.117
  267.3 76.0 %reduce-scatter.3.cloned.1.call-done = bf16[288,768]{1,0:T(8,128)(2,1)} async-done(((bf16[4608,768]{1,0:T(8,128)(2,1)}), bf16[288,768]{1,0:T(8,128)(2,1)}) %reduce-scatter.3.cloned.1.call-update) | async-done | bytes 442384 | tf_op jit(solution)/shard_map/reduce_scatter | solution.py:231
  343.3 155.1 %reduce-scatter.5.cloned.1.call-done = bf16[288,768]{1,0:T(8,128)(2,1)} async-done(((bf16[4608,768]{1,0:T(8,128)(2,1)}), bf16[288,768]{1,0:T(8,128)(2,1)}) %reduce-scatter.5.cloned.1.call-update) | async-done | bytes 442384 | tf_op jit(solution)/shard_map/reduce_scatter | solution.py:231
  498.5 1.8 broadcast_select_fusion.38
  506.1 1.6 maximum_dynamic-update-slice_fusion.4
  512.2 1.8 broadcast_select_fusion.40
  514.0 96.9 %all-reduce.3.cloned.1.call-done = f32[29248]{0:T(1024)} async-done(((f32[29248]{0:T(1024)}), f32[29248]{0:T(1024)}) %all-reduce.3.cloned.1.call-update) | async-done | bytes 117008
  619.5 160.8 %all-gather.4.cloned.1.call-done = bf16[9216,768]{1,0:T(8,128)(2,1)} async-done(((bf16[576,768]{1,0:T(8,128)(2,1)}), bf16[9216,768]{1,0:T(8,128)(2,1)}) %all-gather.4.cloned.1.call-update) | async-done | bytes 14155792 | tf_op jit(solution)/shard_map/all_gather | solution.py:237
  780.2 15.7 %copy.184 = f32[16,2,288,768]{3,2,0,1:T(8,128)} copy(bf16[16,2,288,768]{3,2,1,0:T(8,128)(2,1)} %bitcast.302) | data formatting | bytes 42467328 | tf_op jit(solution)/shard_map/convert_element_type | solution.py:240
  795.9 20.8 %fusion.250 = (f32[2,1536,768]{2,1,0:T(8,128)}, f32[2,1536,768]{2,1,0:T(8,128)}, f32[2,1536,768]{2,1,0:T(8,128)}) fusion(f32[2,4608,768]{2,1,0:T(8,128)} %bitcast.299), kind=kLoop, calls=%fused_computation.396 | loop fusion | bytes 56623104 | tf_op jit(solution)/shard_map/slice | solution.py:244
  816.7 13.5 %copy.186 = f32[768,4,768]{2,1,0:T(4,128)} copy(f32[768,4,768]{2,0,1:T(8,128)} %bitcast.300) | data formatting | bytes 18874368 | tf_op jit(solution)/shard_map/transpose | solution.py:247
  830.1 12.3 %reshape.281 = f32[1,768,3072]{2,1,0:T(8,128)} reshape(f32[768,4,768]{2,1,0:T(4,128)} %copy.186) | data formatting | bytes 18874368 | tf_op jit(solution)/shard_map/reshape | solution.py:247
  842.4 12.4 %reshape.278 = f32[2,2,768,2,384]{4,3,2,1,0:T(2,128)} reshape(f32[2,1536,768]{2,1,0:T(8,128)} %get-tuple-element.101) | data formatting | bytes 18874368 | tf_op jit(solution)/shard_map/reshape | solution.py:248
  854.8 17.1 %copy.185 = f32[2,2,768,2,384]{4,3,2,1,0:T(2,128)} copy(f32[2,2,768,2,384]{4,1,2,0,3:T(2,128)} %bitcast.301) | data formatting | bytes 18874368 | tf_op jit(solution)/shard_map/transpose | solution.py:249
  871.9 13.2 %reshape.279 = f32[4,1,768,768]{3,2,1,0:T(8,128)} reshape(f32[2,2,768,2,384]{4,3,2,1,0:T(2,128)} %copy.185) | data formatting | bytes 18874368 | tf_op jit(solution)/shard_map/reshape | solution.py:249
  885.2 7.6 slice_bitcast_fusion
  (459 shorter events, 96.9 us)
Async XLA Ops:
  7.2 24.7 %copy-start.15 = (bf16[1,768,768]{2,1,0:T(8,128)(2,1)S(1)}, bf16[1,768,768]{2,1,0:T(8,128)(2,1)}, u32[]{:S(2)}) copy-start(bf16[1,768,768]{2,1,0:T(8,128)(2,1)} %param.17) | copy-start | bytes 3538948
  7.2 336.1 %reduce-scatter.3.cloned.1.call-start = ((), (), s32[]{:S(2)}) async-start(), calls=%async_computation.2 | async-start | bytes 7520256 | tf_op jit(solution)/shard_map/reduce_scatter | solution.py:231
  7.3 21.5 %collective-permute-start.4 = (bf16[1,768,768]{2,1,0:T(8,128)(2,1)}, bf16[1,768,768]{2,1,0:T(8,128)(2,1)S(1)}, u32[]{:S(2)}, u32[]{:S(2)}) collective-permute-start(bf16[1,768,768]{2,1,0:T(8,128)(2,1)} %param.16), channel_id=1, source_target_pairs={{0,16},{16,0},{1,17},{17,1},{2,18},{18,2},{3,19},{19,3},{4,20},{20... | collective-permute-start | bytes 3538952 | tf_op jit(solution)/shard_map/ppermute | solution.py:158
  7.8 49.9 %collective-permute-start.8 = (bf16[1,768,3072]{2,1,0:T(8,128)(2,1)}, bf16[1,768,3072]{2,1,0:T(8,128)(2,1)}, u32[]{:S(2)}, u32[]{:S(2)}) collective-permute-start(bf16[1,768,3072]{2,1,0:T(8,128)(2,1)} %param.20), channel_id=1, source_target_pairs={{0,16},{16,0},{1,17},{17,1},{2,18},{18,2},{3,19},{19,3},{4,20},{20... | collective-permute-start | bytes 14155784 | tf_op jit(solution)/shard_map/ppermute | solution.py:158
  7.9 5.1 collective-permute-start.3
  8.3 10.8 %collective-permute-start.2 = (f32[1,12,12]{2,0,1:T(1,128)}, f32[1,12,12]{2,0,1:T(1,128)}, u32[]{:S(2)}, u32[]{:S(2)}) collective-permute-start(f32[1,12,12]{2,0,1:T(1,128)} %param.25), channel_id=1, source_target_pairs={{0,16},{16,0},{1,17},{17,1},{2,18},{18,2},{3,19},{19,3},{4,20},{20... | collective-permute-start | bytes 1736 | tf_op jit(solution)/shard_map/ppermute | solution.py:158
  8.4 23.5 %collective-permute-start.5 = (bf16[1,768,768]{2,1,0:T(8,128)(2,1)}, bf16[1,768,768]{2,1,0:T(8,128)(2,1)S(1)}, u32[]{:S(2)}, u32[]{:S(2)}) collective-permute-start(bf16[1,768,768]{2,1,0:T(8,128)(2,1)} %param.17), channel_id=1, source_target_pairs={{0,16},{16,0},{1,17},{17,1},{2,18},{18,2},{3,19},{19,3},{4,20},{20... | collective-permute-start | bytes 3538952 | tf_op jit(solution)/shard_map/ppermute | solution.py:158
  13.0 12.6 %collective-permute-start = (f32[1,768]{1,0:T(1,128)}, f32[1,768]{1,0:T(1,128)S(1)}, u32[]{:S(2)}, u32[]{:S(2)}) collective-permute-start(f32[1,768]{1,0:T(1,128)} %param.22), channel_id=1, source_target_pairs={{0,16},{16,0},{1,17},{17,1},{2,18},{18,2},{3,19},{19,3},{4,20},{20... | collective-permute-start | bytes 9224 | tf_op jit(solution)/shard_map/ppermute | solution.py:158
  19.0 8.0 collective-permute-start.7
  26.1 20.3 %collective-permute-start.1 = (bf16[1,768,768]{2,1,0:T(8,128)(2,1)}, bf16[1,768,768]{2,1,0:T(8,128)(2,1)}, u32[]{:S(2)}, u32[]{:S(2)}) collective-permute-start(bf16[1,768,768]{2,1,0:T(8,128)(2,1)} %param.18), channel_id=1, source_target_pairs={{0,16},{16,0},{1,17},{17,1},{2,18},{18,2},{3,19},{19,3},{4,20},{20... | collective-permute-start | bytes 3538952 | tf_op jit(solution)/shard_map/ppermute | solution.py:158
  27.0 37.0 %collective-permute-start.9 = (bf16[1,3072,768]{2,1,0:T(8,128)(2,1)}, bf16[1,3072,768]{2,1,0:T(8,128)(2,1)}, u32[]{:S(2)}, u32[]{:S(2)}) collective-permute-start(bf16[1,3072,768]{2,1,0:T(8,128)(2,1)} %param.21), channel_id=1, source_target_pairs={{0,16},{16,0},{1,17},{17,1},{2,18},{18,2},{3,19},{19,3},{4,20},{20... | collective-permute-start | bytes 14155784 | tf_op jit(solution)/shard_map/ppermute | solution.py:158
  28.8 25.8 %collective-permute-start.6 = (bf16[1,768,768]{2,1,0:T(8,128)(2,1)}, bf16[1,768,768]{2,1,0:T(8,128)(2,1)}, u32[]{:S(2)}, u32[]{:S(2)}) collective-permute-start(bf16[1,768,768]{2,1,0:T(8,128)(2,1)} %param.19), channel_id=1, source_target_pairs={{0,16},{16,0},{1,17},{17,1},{2,18},{18,2},{3,19},{19,3},{4,20},{20... | collective-permute-start | bytes 3538952 | tf_op jit(solution)/shard_map/ppermute | solution.py:158
  47.3 7.3 copy-start.38
  47.3 7.3 copy-start.115
  53.6 121.9 %collective-permute-start.20 = (bf16[256,768]{0,1:T(8,128)(2,1)}, bf16[256,768]{0,1:T(8,128)(2,1)}, u32[]{:S(2)}, u32[]{:S(2)}) collective-permute-start(bf16[256,768]{0,1:T(8,128)(2,1)} %bitcast.10), channel_id=1, source_target_pairs={{0,16},{16,0},{1,17},{17,1},{2,18},{18,2},{3,19},{19,3},{4,20},{20... | collective-permute-start | bytes 1179656 | tf_op jit(solution)/shard_map/ppermute | solution.py:158
  56.9 7.1 copy-start.34
  57.5 6.5 copy-start.100
  57.5 6.5 slice-start
  80.8 9.3 %slice-start.6 = ((s8[4718592]{0:T(1024)(128)(4,1)}), s8[4194304]{0:T(1024)(128)(4,1)S(1)}, s32[]{:S(2)}) async-start(s8[4718592]{0:T(1024)(128)(4,1)} %bitcast.341), calls=%async_computation.12 | async-start | bytes 8388608
  83.2 6.8 slice-start.7
  87.1 7.3 slice-start.2
  94.4 11.1 %copy-start.47 = (bf16[256,3072]{1,0:T(8,128)(2,1)}, bf16[256,3072]{1,0:T(8,128)(2,1)S(1)}, u32[]{:S(2)}) copy-start(bf16[256,3072]{1,0:T(8,128)(2,1)S(1)} %get-tuple-element.167) | copy-start | bytes 4718596
  119.1 14.3 %copy-start.27 = (bf16[12,64,256]{2,1,0:T(8,128)(2,1)}, bf16[12,64,256]{2,1,0:T(8,128)(2,1)S(1)}, u32[]{:S(2)}) copy-start(bf16[12,64,256]{2,1,0:T(8,128)(2,1)S(1)} %convolution_convert_fusion.14) | copy-start | bytes 1179652
  121.0 6.7 copy-start.31
  121.1 6.7 copy-start.104
  139.3 7.9 copy-start.8
  156.7 7.0 copy-start.32
  156.7 7.0 copy-start.102
  169.4 11.9 %collective-permute-start.15 = (bf16[256,1536]{1,0:T(8,128)(2,1)S(1)}, bf16[256,1536]{1,0:T(8,128)(2,1)S(1)}, u32[]{:S(2)}, u32[]{:S(2)}) collective-permute-start(bf16[256,1536]{1,0:T(8,128)(2,1)S(1)} %copy-done.67), channel_id=1, source_target_pairs={{0,16},{16,0},{1,17},{17,1},{2,18},{18,2},{3,19},{19,3},{4,20},{20... | collective-permute-start | bytes 2359304 | tf_op jit(solution)/shard_map/ppermute | solution.py:158
  173.7 5.0 collective-permute-start.16
  174.9 1.5 collective-permute-start.21
  174.9 1.8 collective-permute-start.18
  175.5 7.3 collective-permute-start.12
  176.4 4.9 collective-permute-start.14
  176.8 2.9 collective-permute-start.19
  178.8 1.9 collective-permute-start.17
  179.7 3.1 collective-permute-start.13
  190.1 308.4 %reduce-scatter.5.cloned.1.call-start = ((), (), s32[]{:S(2)}) async-start(), calls=%async_computation.3 | async-start | bytes 7520256 | tf_op jit(solution)/shard_map/reduce_scatter | solution.py:231
  190.1 7.7 collective-permute-start.26
  191.7 4.0 collective-permute-start.31
  193.1 2.9 collective-permute-start.29
  194.9 6.7 collective-permute-start.25
  195.3 2.2 collective-permute-start.28
  195.7 5.3 collective-permute-start.30
  196.0 7.0 collective-permute-start.22
  197.5 4.1 collective-permute-start.24
  197.8 2.2 collective-permute-start.27
  200.0 3.0 collective-permute-start.23
  210.3 400.6 %all-reduce.3.cloned.1.call-start = ((), (), s32[]{:S(2)}) async-start(), calls=%async_computation.5 | async-start | bytes 237568
  222.1 15.6 %copy-start.112 = (f32[768]{0:T(1024)S(1)}, f32[768]{0:T(1024)}, u32[]{:S(2)}) copy-start(f32[768]{0:T(1024)} %get-tuple-element.69) | copy-start | bytes 9220
  240.4 10.1 %copy-start.3 = (f32[12,256,256]{2,1,0:T(8,128)S(1)}, f32[12,256,256]{2,1,0:T(8,128)}, u32[]{:S(2)}) copy-start(f32[12,256,256]{2,1,0:T(8,128)} %copy-done.2) | copy-start | bytes 9437188
  267.3 242.9 %copy-start.54 = (bf16[256,768]{1,0:T(8,128)(2,1)S(1)}, bf16[256,768]{1,0:T(8,128)(2,1)}, u32[]{:S(2)}) copy-start(bf16[256,768]{1,0:T(8,128)(2,1)} %get-tuple-element.123) | copy-start | bytes 1179652
  500.3 7.7 collective-permute-start.32
  500.4 5.0 collective-permute-start.33
  502.2 1.9 collective-permute-start.34
  505.4 6.8 copy-start.9
  505.4 6.8 copy-start.30
  505.4 6.8 copy-start.33
  505.4 6.8 copy-start.40
  505.4 6.8 copy-start.99
  507.7 272.5 %all-gather.4.cloned.1.call-start = ((), (), s32[]{:S(2)}) async-start(), calls=%async_computation.4 | async-start | bytes 15040512 | tf_op jit(solution)/shard_map/all_gather | solution.py:237
  511.0 105.4 %collective-permute-start.10 = (bf16[256,768]{1,0:T(8,128)(2,1)}, bf16[256,768]{1,0:T(8,128)(2,1)}, u32[]{:S(2)}, u32[]{:S(2)}) collective-permute-start(bf16[256,768]{1,0:T(8,128)(2,1)} %broadcast_select_fusion.42), channel_id=1, source_target_pairs={{0,16},{16,0},{1,17},{17,1},{2,18},{18,2},{3,19},{19,3},{4,20},{20... | collective-permute-start | bytes 1179656 | tf_op jit(solution)/shard_map/ppermute | solution.py:158
  514.0 104.5 %collective-permute-start.11 = (bf16[256,768]{1,0:T(8,128)(2,1)}, bf16[256,768]{1,0:T(8,128)(2,1)S(1)}, u32[]{:S(2)}, u32[]{:S(2)}) collective-permute-start(bf16[256,768]{1,0:T(8,128)(2,1)} %get-tuple-element.85), channel_id=1, source_target_pairs={{0,16},{16,0},{1,17},{17,1},{2,18},{18,2},{3,19},{19,3},{4,20},{20... | collective-permute-start | bytes 1179656 | tf_op jit(solution)/shard_map/ppermute | solution.py:158
  885.2 7.6 copy-start.1
  (111 other events, 385.7 us)
Sparse Core Ops, SparseCore 0:
  190.2 153.1 reduce-scatter.2
  349.2 149.1 reduce-scatter.4
  507.8 103.0 all-reduce.2
  614.1 166.0 all-gather.3
